TPU v7x, 256 devices: a whole 4x4x8 slice. The times are simulated.
256 devices in a mesh: col: 32 (over x, y, core), sub: 8 (over z).
Axes of the slice: x: 4, y: 4, z: 8, core: 2. Of those that a mesh axis runs over, the one named last changes fastest.
Arguments:
- vectors: bfloat16 [1048576, 128], P(('col', 'sub')), may hold values from -6 to 6
- near_blocks: bfloat16 [4096, 4, 256, 256], P(('col', 'sub')), may hold values from -0.1875 to 0.1875
- near_index: int32 [4096, 4], P(('col', 'sub')), may hold values from 0 to 4095, as said below
- leaf_basis: bfloat16 [4096, 32, 256], P(('col', 'sub')), may hold values from -0.375 to 0.375
- leaf_transfer: float32 [4096, 32, 32], P(('col', 'sub')), may hold values from -0.25 to 0.25
- leaf_coupling: float32 [4096, 8, 32, 32], P(('col', 'sub')), may hold values from -0.375 to 0.375
- leaf_far: int32 [4096, 8], P(('col', 'sub')), may hold values from 0 to 4095, as said below
- cluster_transfer: float32 [256, 32, 32], P(('col', 'sub')), may hold values from -0.375 to 0.375
- cluster_coupling: float32 [256, 4, 32, 32], P(('col', 'sub')), may hold values from -0.5 to 0.5
- cluster_partner: int32 [256, 4], P(('col', 'sub')), may hold values from 0 to 7
- top_coupling: float32 [32, 8, 32, 32], P('col'), may hold values from -0.375 to 0.375
- top_partner: int32 [32, 8], P('col'), may hold values from 0 to 31
Outputs:
- products: bfloat16 [1048576, 128], P(('col', 'sub'))
Inputs may be any that keep to these rules, and one draw needn't show every extreme that they name: `near_index`: slot 0 of leaf i is i itself; every entry lies within 16 leaves of i; slot 1 is exactly 16 leaves away from i. `leaf_far`: every entry lies within 16 leaves of its row leaf i; slots 0 and 1 are exactly 16 leaves away from i.
All inputs are finite; a program needn't handle non-finite values.
Results may differ from a plain program's by a relative error of at most 0.0034.
Values may be sent and summed in bfloat16 or wider, within the bound.
A program may use at most 64 MiB of HBM per device.

v0:
```python
import jax
import jax.numpy as jnp
from jax import lax
from jax.sharding import PartitionSpec as P

HIGHEST = lax.Precision.HIGHEST


def with_halo(block, sides, width):
    for axis, dim in sides:
        count = lax.axis_size(axis)
        forward = [(i, i + 1) for i in range(count - 1)]
        backward = [(target, source) for source, target in forward]
        low = lax.ppermute(
            lax.slice_in_dim(block, block.shape[dim] - width, None, axis=dim), axis, forward
        )
        high = lax.ppermute(lax.slice_in_dim(block, 0, width, axis=dim), axis, backward)
        block = jnp.concatenate([low, block, high], axis=dim)
    return block


def local(
    vectors,
    near_blocks,
    near_index,
    leaf_basis,
    leaf_transfer,
    leaf_coupling,
    leaf_far,
    cluster_transfer,
    cluster_coupling,
    cluster_partner,
    top_coupling,
    top_partner,
):
    leaves_here = leaf_basis.shape[0]
    leaf_rows = leaf_basis.shape[2]
    columns = vectors.shape[1]
    window_start = lax.axis_index(("col", "sub")) * leaves_here - leaves_here
    widened = with_halo(vectors, ((("col", "sub"), 0),), leaves_here * leaf_rows)
    window_vec = widened.reshape(3 * leaves_here, leaf_rows, columns)
    own_vec = vectors.reshape(leaves_here, leaf_rows, columns)
    leaf_coefs = jnp.einsum("lrp,lpc->lrc", leaf_basis, own_vec, preferred_element_type=jnp.float32)
    window_coefs = with_halo(leaf_coefs, ((("col", "sub"), 0),), leaves_here)
    cluster_coef = jnp.einsum("lrs,lrc->sc", leaf_transfer, leaf_coefs, precision=HIGHEST)
    sub_coefs = lax.all_gather(cluster_coef[None], "sub", axis=0, tiled=True)
    cluster_field = jnp.einsum(
        "krs,ksc->rc", cluster_coupling[0], sub_coefs[cluster_partner[0]], precision=HIGHEST
    )
    upward = jnp.dot(cluster_transfer[0].T, cluster_coef, precision=HIGHEST)
    top_coef = lax.psum(upward, "sub")
    col_coefs = lax.all_gather(top_coef[None], "col", axis=0, tiled=True)
    top_field = jnp.einsum(
        "krs,ksc->rc", top_coupling[0], col_coefs[top_partner[0]], precision=HIGHEST
    )
    cluster_field = cluster_field + jnp.dot(cluster_transfer[0], top_field, precision=HIGHEST)
    far_coefs = window_coefs[leaf_far - window_start]
    leaf_field = jnp.einsum("lkrs,lksc->lrc", leaf_coupling, far_coefs, precision=HIGHEST)
    leaf_field = leaf_field + jnp.einsum(
        "lrs,sc->lrc", leaf_transfer, cluster_field, precision=HIGHEST
    )
    rounded = leaf_field.astype(jnp.bfloat16)
    picked = window_vec[near_index - window_start]
    near_part = jnp.einsum(
        "lkij,lkjc->lic", near_blocks, picked, preferred_element_type=jnp.float32
    )
    far_part = jnp.einsum("lrp,lrc->lpc", leaf_basis, rounded, preferred_element_type=jnp.float32)
    return (near_part + far_part).astype(jnp.bfloat16).reshape(leaves_here * leaf_rows, columns)


def solution(mesh):
    in_specs = (
        P(("col", "sub"), None),
        P(("col", "sub"), None, None, None),
        P(("col", "sub"), None),
        P(("col", "sub"), None, None),
        P(("col", "sub"), None, None),
        P(("col", "sub"), None, None, None),
        P(("col", "sub"), None),
        P(("col", "sub"), None, None),
        P(("col", "sub"), None, None, None),
        P(("col", "sub"), None),
        P("col", None, None, None),
        P("col", None),
    )
    out_specs = P(("col", "sub"), None)
    return jax.shard_map(local, mesh=mesh, in_specs=in_specs, out_specs=out_specs, check_vma=False)
```

profile of v0, /device:TPU:1, one launch (start us, length us, event | category | flops | bytes accessed | tf_op | source)
XLA Modules:
  0.0 154.2 jit_solution(7868082268854348627)
XLA Ops:
  0.0 0.0 copy-start
  0.0 0.0 copy-start.5
  0.0 0.0 copy-start.4
  0.0 1.7 %fusion.12 = f32[16,32,128]{2,1,0:T(8,128)S(1)} fusion(bf16[16,32,256]{2,1,0:T(8,128)(2,1)} %param.15, bf16[16,256,128]{2,1,0:T(8,128)(2,1)} %bitcast.79), kind=kOutput, calls=%fused_computation.33 | convolution fusion | flops 33554432 | bytes 1572864 | tf_op jit(solution)/shard_map/lrp,lpc->lrc/dot_general | solution.py:43
  1.7 8.9 %collective-permute-start.3 = (f32[16,32,128]{2,1,0:T(8,128)S(1)}, f32[16,32,128]{2,1,0:T(8,128)S(1)}, u32[]{:S(2)}, u32[]{:S(2)}) collective-permute-start(f32[16,32,128]{2,1,0:T(8,128)S(1)} %fusion.12), channel_id=1, source_target_pairs={{1,0},{2,1},{3,2},{4,3},{5,4},{6,5},{7,6},{8,7},{9,8},{10,9},{11,1... | collective-permute-start | bytes 786440 | tf_op jit(solution)/shard_map/ppermute | solution.py:17
  10.6 1.9 %collective-permute-start.2 = (f32[16,32,128]{2,1,0:T(8,128)S(1)}, f32[16,32,128]{2,1,0:T(8,128)}, u32[]{:S(2)}, u32[]{:S(2)}) collective-permute-start(f32[16,32,128]{2,1,0:T(8,128)S(1)} %fusion.12), channel_id=1, source_target_pairs={{0,1},{1,2},{2,3},{3,4},{4,5},{5,6},{6,7},{7,8},{8,9},{9,10},{10,1... | collective-permute-start | bytes 786440 | tf_op jit(solution)/shard_map/ppermute | solution.py:14
  12.5 4.9 %collective-permute-start.1 = (bf16[4096,128]{1,0:T(8,128)(2,1)}, bf16[4096,128]{1,0:T(8,128)(2,1)}, u32[]{:S(2)}, u32[]{:S(2)}) collective-permute-start(bf16[4096,128]{1,0:T(8,128)(2,1)} %param.12), channel_id=1, source_target_pairs={{1,0},{2,1},{3,2},{4,3},{5,4},{6,5},{7,6},{8,7},{9,8},{10,9},{11,1... | collective-permute-start | bytes 3145736 | tf_op jit(solution)/shard_map/ppermute | solution.py:17
  17.4 1.9 %collective-permute-start = (bf16[4096,128]{1,0:T(8,128)(2,1)}, bf16[4096,128]{1,0:T(8,128)(2,1)}, u32[]{:S(2)}, u32[]{:S(2)}) collective-permute-start(bf16[4096,128]{1,0:T(8,128)(2,1)} %param.12), channel_id=1, source_target_pairs={{0,1},{1,2},{2,3},{3,4},{4,5},{5,6},{6,7},{7,8},{8,9},{9,10},{10,1... | collective-permute-start | bytes 3145736 | tf_op jit(solution)/shard_map/ppermute | solution.py:14
  19.3 0.7 fusion.10
  20.0 0.7 fusion.11
  20.7 1.3 compare_select_fusion.1
  21.9 0.7 compare_select_fusion
  22.6 0.6 pad_clamp_fusion
  23.2 0.1 copy.24
  23.3 0.6 reshape.78
  23.9 1.5 fusion.13
  25.4 0.9 convolution_bitcast_fusion.3
  26.4 35.0 %psum.7 = f32[1,32,128]{2,1,0:T(8,128)S(1)} all-reduce(f32[1,32,128]{2,1,0:T(8,128)S(1)} %convolution_bitcast_fusion.3), channel_id=1, replica_groups=mesh['col'=32,'sub'=8] {'sub'}, use_global_device_ids=true, to_apply=%region_0.0 | all-reduce | flops 4096 | bytes 32768 | tf_op jit(solution)/shard_map/psum | solution.py:51
  61.4 18.5 %all-gather = f32[256,128]{1,0:T(8,128)S(1)} all-gather(f32[32,128]{1,0:T(8,128)S(1)} %bitcast.81), channel_id=2, replica_groups=mesh['col'=32,'sub'=8] {'sub'}, dimensions={0}, use_global_device_ids=true | all-gather | bytes 147456 | tf_op jit(solution)/shard_map/all_gather | solution.py:46
  79.9 36.2 %all_gather.7 = f32[32,32,128]{2,1,0:T(8,128)S(1)} all-gather(f32[1,32,128]{2,1,0:T(8,128)S(1)} %psum.7), channel_id=1, replica_groups=mesh['col'=32,'sub'=8] {'col'}, dimensions={0}, use_global_device_ids=true | all-gather | bytes 540672 | tf_op jit(solution)/shard_map/all_gather | solution.py:52
  116.1 0.6 gather_fusion.2
  116.6 0.0 copy-done.5
  116.6 0.2 convolution_bitcast_fusion.4
  116.9 0.7 gather_fusion.3
  117.6 0.0 copy-done.4
  117.6 0.3 convolution_bitcast_fusion.2
  117.9 0.6 pad_clamp_fusion.2
  118.5 0.7 copy.22
  119.3 0.1 reshape.70
  119.4 0.9 fusion.4
  120.2 0.0 collective-permute-done.3
  120.3 0.0 collective-permute-done.2
  120.3 1.0 pad_maximum_fusion.1
  121.3 2.1 %gather_fusion.1 = f32[128,32,128]{2,1,0:T(8,128)} fusion(f32[48,32,128]{2,1,0:T(8,128)S(1)} %pad_maximum_fusion.1, s32[1024]{0:T(1024)S(1)} %pad_clamp_fusion.2), kind=kCustom, calls=%fused_computation.1 | custom fusion | bytes 4194816 | tf_op jit(solution)/shard_map/gather | solution.py:57
  123.4 0.0 copy-start.3
  123.4 0.0 copy-done
  123.4 4.4 %convolution_bitcast_fusion.1 = f32[16,32,128]{2,1,0:T(8,128)S(1)} fusion(f32[16,8,32,128]{3,2,1,0:T(8,128)} %bitcast.78, f32[16,8,32,32]{3,2,1,0:T(8,128)S(1)} %copy-done), kind=kOutput, calls=%fused_computation.10 | convolution fusion | flops 201326592 | bytes 2883584 | tf_op jit(solution)/shard_map/lkrs,lksc->lrc/dot_general | solution.py:58
  127.9 0.0 copy-done.3
  127.9 0.4 fusion.3
  128.2 0.0 copy-done.2
  128.2 1.9 %fusion.14 = f32[16,128,256]{2,1,0:T(8,128)} fusion(bf16[16,32,128]{2,1,0:T(8,128)(2,1)S(1)} %fusion.3, bf16[16,32,256]{2,1,0:T(8,128)(2,1)S(1)} %copy-done.2), kind=kOutput, calls=%fused_computation.35 | convolution fusion | flops 33554432 | bytes 2490368 | tf_op jit(solution)/shard_map/lrp,lrc->lpc/dot_general | solution.py:67
  130.1 0.0 collective-permute-done.1
  130.1 0.0 collective-permute-done
  130.1 0.0 copy-done.1
  130.1 9.8 %pad_maximum_fusion = bf16[12288,128]{1,0:T(8,128)(2,1)} fusion(bf16[4096,128]{1,0:T(8,128)(2,1)} %collective-permute-done.1, bf16[4096,128]{1,0:T(8,128)(2,1)S(1)} %copy-done.1, bf16[4096,128]{1,0:T(8,128)(2,1)} %collective-permute-done), kind=kLoop, calls=%fused_computation.4 | loop fusion | flops 9437184 | bytes 6291456 | tf_op jit(solution)/shard_map/concatenate | solution.py:18
  139.9 4.9 %gather_fusion = bf16[64,256,128]{2,1,0:T(8,128)(2,1)} fusion(bf16[48,256,128]{2,1,0:T(8,128)(2,1)} %bitcast.76, s32[1024]{0:T(1024)S(1)} %pad_clamp_fusion.3), kind=kCustom, calls=%fused_computation | custom fusion | bytes 8388864 | tf_op jit(solution)/shard_map/gather | solution.py:63
  144.8 8.1 %fusion.1 = bf16[16,256,128]{1,2,0:T(8,128)(2,1)S(1)} fusion(f32[16,128,256]{2,1,0:T(8,128)} %fusion.14, bf16[16,4,256,128]{3,2,1,0:T(8,128)(2,1)} %bitcast.77, bf16[16,4,256,256]{3,2,1,0:T(8,128)(2,1)} %param.13), kind=kOutput, calls=%fused_computation.7 | convolution fusion | flops 1074790400 | bytes 15728640 | tf_op jit(solution)/shard_map/lkij,lkjc->lic/dot_general | solution.py:64
  152.9 1.3 copy.26
  (4 shorter events, 0.0 us)
Async XLA Ops:
  0.0 123.4 %copy-start = (f32[16,8,32,32]{3,2,1,0:T(8,128)S(1)}, f32[16,8,32,32]{3,2,1,0:T(8,128)}, u32[]{:S(2)}) copy-start(f32[16,8,32,32]{3,2,1,0:T(8,128)} %param.17) | copy-start | bytes 1572868
  0.0 116.6 %copy-start.5 = (f32[1,4,32,32]{3,2,1,0:T(8,128)S(1)}, f32[1,4,32,32]{3,2,1,0:T(8,128)}, u32[]{:S(2)}) copy-start(f32[1,4,32,32]{3,2,1,0:T(8,128)} %param.20) | copy-start | bytes 49156
  0.0 117.6 %copy-start.4 = (f32[1,8,32,32]{3,2,1,0:T(8,128)S(1)}, f32[1,8,32,32]{3,2,1,0:T(8,128)}, u32[]{:S(2)}) copy-start(f32[1,8,32,32]{3,2,1,0:T(8,128)} %param.22) | copy-start | bytes 98308
  1.7 118.5 %collective-permute-start.3 = (f32[16,32,128]{2,1,0:T(8,128)S(1)}, f32[16,32,128]{2,1,0:T(8,128)S(1)}, u32[]{:S(2)}, u32[]{:S(2)}) collective-permute-start(f32[16,32,128]{2,1,0:T(8,128)S(1)} %fusion.12), channel_id=1, source_target_pairs={{1,0},{2,1},{3,2},{4,3},{5,4},{6,5},{7,6},{8,7},{9,8},{10,9},{11,1... | collective-permute-start | bytes 786440 | tf_op jit(solution)/shard_map/ppermute | solution.py:17
  10.6 109.6 %collective-permute-start.2 = (f32[16,32,128]{2,1,0:T(8,128)S(1)}, f32[16,32,128]{2,1,0:T(8,128)}, u32[]{:S(2)}, u32[]{:S(2)}) collective-permute-start(f32[16,32,128]{2,1,0:T(8,128)S(1)} %fusion.12), channel_id=1, source_target_pairs={{0,1},{1,2},{2,3},{3,4},{4,5},{5,6},{6,7},{7,8},{8,9},{9,10},{10,1... | collective-permute-start | bytes 786440 | tf_op jit(solution)/shard_map/ppermute | solution.py:14
  12.5 117.6 %collective-permute-start.1 = (bf16[4096,128]{1,0:T(8,128)(2,1)}, bf16[4096,128]{1,0:T(8,128)(2,1)}, u32[]{:S(2)}, u32[]{:S(2)}) collective-permute-start(bf16[4096,128]{1,0:T(8,128)(2,1)} %param.12), channel_id=1, source_target_pairs={{1,0},{2,1},{3,2},{4,3},{5,4},{6,5},{7,6},{8,7},{9,8},{10,9},{11,1... | collective-permute-start | bytes 3145736 | tf_op jit(solution)/shard_map/ppermute | solution.py:17
  17.4 112.7 %collective-permute-start = (bf16[4096,128]{1,0:T(8,128)(2,1)}, bf16[4096,128]{1,0:T(8,128)(2,1)}, u32[]{:S(2)}, u32[]{:S(2)}) collective-permute-start(bf16[4096,128]{1,0:T(8,128)(2,1)} %param.12), channel_id=1, source_target_pairs={{0,1},{1,2},{2,3},{3,4},{4,5},{5,6},{6,7},{7,8},{8,9},{9,10},{10,1... | collective-permute-start | bytes 3145736 | tf_op jit(solution)/shard_map/ppermute | solution.py:14
  123.4 4.4 %copy-start.3 = (f32[16,32,32]{2,1,0:T(8,128)S(1)}, f32[16,32,32]{2,1,0:T(8,128)}, u32[]{:S(2)}) copy-start(f32[16,32,32]{2,1,0:T(8,128)} %param.16) | copy-start | bytes 196612
  123.4 4.8 %copy-start.2 = (bf16[16,32,256]{2,1,0:T(8,128)(2,1)S(1)}, bf16[16,32,256]{2,1,0:T(8,128)(2,1)}, u32[]{:S(2)}) copy-start(bf16[16,32,256]{2,1,0:T(8,128)(2,1)} %param.15) | copy-start | bytes 786436
  123.4 6.7 %copy-start.1 = (bf16[4096,128]{1,0:T(8,128)(2,1)S(1)}, bf16[4096,128]{1,0:T(8,128)(2,1)}, u32[]{:S(2)}) copy-start(bf16[4096,128]{1,0:T(8,128)(2,1)} %param.12) | copy-start | bytes 3145732
where the time goes:
time: 155 us; the launch traced here: 154 us
  blocking collectives  89.7 us (58%)
  matrix products  20.3 us (13%)
  starting transfers between devices  17.6 us (11%)
  other arithmetic  15.3 us (10%)
  local copies, waits for them, and re-layouts  11.1 us (7%)
    all_gather x1, blocking collectives, local(): col_coefs = lax.all_gather(top_coef[None], 'col', axis=0, tiled=True)  36.2 us
    psum x1, blocking collectives, local(): top_coef = lax.psum(upward, 'sub')  35 us
    all_gather x1, blocking collectives, local(): sub_coefs = lax.all_gather(cluster_coef[None], 'sub', axis=0, tiled=True)  18.5 us
    ppermute x2, starting transfers between devices, with_halo(): lax.ppermute(lax.slice_in_dim(block, 0, width, axis=dim), axis, backward)  13.7 us
    concatenate x2, other arithmetic, with_halo(): block = jnp.concatenate([low, block, high], axis=dim)  10.8 us
    dot_general x1, matrix products, local(): jnp.einsum('lkij,lkjc->lic', near_blocks, picked, preferred_element_type=...  8.06 us
    gather x1, local copies, waits for them, and re-layouts, local(): picked = window_vec[near_index - window_start]  4.91 us
    dot_general x1, matrix products, local(): jnp.einsum('lkrs,lksc->lrc', leaf_coupling, far_coefs, precision=HIGHEST)  4.43 us
  transfers between devices with their start and end apart: 4, of which 0 were waited for; matrix products, arithmetic and copies ran while one was open for 14% of the time, Pallas kernels for 0%

commit v1 on v0

--- a/solution.py
+++ b/solution.py
@@ -48,7 +48,9 @@
         "krs,ksc->rc", cluster_coupling[0], sub_coefs[cluster_partner[0]], precision=HIGHEST
     )
     upward = jnp.dot(cluster_transfer[0].T, cluster_coef, precision=HIGHEST)
-    top_coef = lax.psum(upward, "sub")
+    top_coef = upward
+    for hop in (1, 2, 4):
+        top_coef = top_coef + lax.ppermute(top_coef, "sub", [(dev, dev ^ hop) for dev in range(8)])
     col_coefs = lax.all_gather(top_coef[None], "col", axis=0, tiled=True)
     top_field = jnp.einsum(
         "krs,ksc->rc", top_coupling[0], col_coefs[top_partner[0]], precision=HIGHEST

time: 155 us -> 142 us (0.916)
  blocking collectives: 89.7 us -> 67.7 us
  waiting for transfers between devices: 0.01 us -> 8.63 us
  matrix products: 20.3 us -> 22.3 us
  other arithmetic: 15.3 us -> 13.5 us
    psum x1 -> x0, blocking collectives: 35 us -> none  [local(): top_coef = lax.psum(upward, 'sub')]
    all_gather x1, blocking collectives: 18.5 us -> 35.9 us  [local(): sub_coefs = lax.all_gather(cluster_coef[None], 'sub', axis=0, tiled=True)]
    ppermute x0 -> x3, waiting for transfers between devices: none -> 8.62 us  [local(): lax.ppermute(top_coef, 'sub', [(dev, dev ^ hop) for dev in range(8)])]
    all_gather x1, blocking collectives: 36.2 us -> 31.8 us  [local(): col_coefs = lax.all_gather(top_coef[None], 'col', axis=0, tiled=True)]
  transfers between devices with their start and end apart: 4 -> 7, of which waited for: 0 -> 2; matrix products, arithmetic and copies ran while one was open for 14% -> 14% of each run, Pallas kernels for 0% -> 0%
where the time goes in v1:
time: 142 us; the launch traced here: 141 us
  blocking collectives  67.7 us (48%)
  matrix products  22.3 us (16%)
  starting transfers between devices  18.9 us (13%)
  other arithmetic  13.5 us (10%)
  local copies, waits for them, and re-layouts  9.81 us (7%)
  waiting for transfers between devices  8.63 us (6%)
    all_gather x1, blocking collectives, local(): sub_coefs = lax.all_gather(cluster_coef[None], 'sub', axis=0, tiled=True)  35.9 us
    all_gather x1, blocking collectives, local(): col_coefs = lax.all_gather(top_coef[None], 'col', axis=0, tiled=True)  31.8 us
    ppermute x2, starting transfers between devices, with_halo(): lax.ppermute(lax.slice_in_dim(block, 0, width, axis=dim), axis, backward)  13.7 us
    concatenate x2, other arithmetic, with_halo(): block = jnp.concatenate([low, block, high], axis=dim)  10.8 us
    ppermute x3, waiting for transfers between devices, local(): lax.ppermute(top_coef, 'sub', [(dev, dev ^ hop) for dev in range(8)])  8.62 us
    dot_general x1, matrix products, local(): jnp.einsum('lkij,lkjc->lic', near_blocks, picked, preferred_element_type=...  8.07 us
    gather x1, local copies, waits for them, and re-layouts, local(): picked = window_vec[near_index - window_start]  4.93 us
    dot_general x1, matrix products, local(): jnp.einsum('lkrs,lksc->lrc', leaf_coupling, far_coefs, precision=HIGHEST)  4.43 us
  transfers between devices with their start and end apart: 7, of which 2 were waited for; matrix products, arithmetic and copies ran while one was open for 14% of the time, Pallas kernels for 0%

profile of v1, /device:TPU:1, one launch (start us, length us, event | category | flops | bytes accessed | tf_op | source)
XLA Modules:
  0.0 141.1 jit_solution(11692562266316405104)
XLA Ops:
  0.0 0.0 copy-start
  0.0 0.0 copy-start.4
  0.0 1.7 %fusion.12 = f32[16,32,128]{2,1,0:T(8,128)S(1)} fusion(bf16[16,32,256]{2,1,0:T(8,128)(2,1)} %param.15, bf16[16,256,128]{2,1,0:T(8,128)(2,1)} %bitcast.78), kind=kOutput, calls=%fused_computation.33 | convolution fusion | flops 33554432 | bytes 1572864 | tf_op jit(solution)/shard_map/lrp,lpc->lrc/dot_general | solution.py:43
  1.7 8.9 %collective-permute-start.3 = (f32[16,32,128]{2,1,0:T(8,128)S(1)}, f32[16,32,128]{2,1,0:T(8,128)S(1)}, u32[]{:S(2)}, u32[]{:S(2)}) collective-permute-start(f32[16,32,128]{2,1,0:T(8,128)S(1)} %fusion.12), channel_id=1, source_target_pairs={{1,0},{2,1},{3,2},{4,3},{5,4},{6,5},{7,6},{8,7},{9,8},{10,9},{11,1... | collective-permute-start | bytes 786440 | tf_op jit(solution)/shard_map/ppermute | solution.py:17
  10.6 1.9 %collective-permute-start.2 = (f32[16,32,128]{2,1,0:T(8,128)S(1)}, f32[16,32,128]{2,1,0:T(8,128)}, u32[]{:S(2)}, u32[]{:S(2)}) collective-permute-start(f32[16,32,128]{2,1,0:T(8,128)S(1)} %fusion.12), channel_id=1, source_target_pairs={{0,1},{1,2},{2,3},{3,4},{4,5},{5,6},{6,7},{7,8},{8,9},{9,10},{10,1... | collective-permute-start | bytes 786440 | tf_op jit(solution)/shard_map/ppermute | solution.py:14
  12.5 4.9 %collective-permute-start.1 = (bf16[4096,128]{1,0:T(8,128)(2,1)}, bf16[4096,128]{1,0:T(8,128)(2,1)}, u32[]{:S(2)}, u32[]{:S(2)}) collective-permute-start(bf16[4096,128]{1,0:T(8,128)(2,1)} %param.12), channel_id=1, source_target_pairs={{1,0},{2,1},{3,2},{4,3},{5,4},{6,5},{7,6},{8,7},{9,8},{10,9},{11,1... | collective-permute-start | bytes 3145736 | tf_op jit(solution)/shard_map/ppermute | solution.py:17
  17.4 1.9 %collective-permute-start = (bf16[4096,128]{1,0:T(8,128)(2,1)}, bf16[4096,128]{1,0:T(8,128)(2,1)}, u32[]{:S(2)}, u32[]{:S(2)}) collective-permute-start(bf16[4096,128]{1,0:T(8,128)(2,1)} %param.12), channel_id=1, source_target_pairs={{0,1},{1,2},{2,3},{3,4},{4,5},{5,6},{6,7},{7,8},{8,9},{9,10},{10,1... | collective-permute-start | bytes 3145736 | tf_op jit(solution)/shard_map/ppermute | solution.py:14
  19.3 1.5 %fusion.13 = f32[128,32,1]{0,1,2:T(8,128)S(1)} fusion(f32[16,32,128]{2,1,0:T(8,128)S(1)} %fusion.12, f32[16,32,32]{2,1,0:T(8,128)} %param.16), kind=kOutput, calls=%fused_computation.34 | convolution fusion | flops 25165824 | bytes 344064 | tf_op jit(solution)/shard_map/lrs,lrc->sc/dot_general | solution.py:45
  20.9 0.9 convolution_bitcast_fusion.4
  21.8 0.1 collective-permute-start.4
  21.9 0.7 fusion.10
  22.6 0.7 fusion.11
  23.2 0.7 compare_select_fusion.1
  23.9 0.7 compare_select_fusion
  24.6 35.9 %all-gather = f32[256,128]{1,0:T(8,128)S(1)} all-gather(f32[32,128]{1,0:T(8,128)S(1)} %bitcast.81), channel_id=2, replica_groups=mesh['col'=32,'sub'=8] {'sub'}, dimensions={0}, use_global_device_ids=true | all-gather | bytes 147456 | tf_op jit(solution)/shard_map/all_gather | solution.py:46
  60.5 0.6 gather_fusion.2
  61.1 1.4 %convolution_bitcast_fusion.3 = f32[128,32]{1,0:T(8,128)S(1)} fusion(f32[4,32,128]{2,1,0:T(8,128)S(1)} %gather_fusion.2, f32[1,4,32,32]{3,2,1,0:T(8,128)} %param.20), kind=kOutput, calls=%fused_computation.15 | convolution fusion | flops 6291456 | bytes 98304 | tf_op jit(solution)/shard_map/krs,ksc->rc/dot_general | solution.py:47
  62.5 0.1 copy.19
  62.6 0.1 reshape.78
  62.7 0.0 collective-permute-done.4
  62.7 0.1 collective-permute-start.5
  62.8 0.1 copy.17
  62.9 0.1 reshape.70
  63.0 3.3 %collective-permute-done.5 = f32[32,128]{1,0:T(8,128)S(1)} collective-permute-done((f32[32,128]{1,0:T(8,128)S(1)}, f32[32,128]{1,0:T(8,128)S(1)}, u32[]{:S(2)}, u32[]{:S(2)}) %collective-permute-start.5) | collective-permute-done | bytes 16416 | tf_op jit(solution)/shard_map/ppermute | solution.py:53
  66.3 1.2 collective-permute-start.6
  67.5 5.3 %collective-permute-done.6 = f32[32,128]{1,0:T(8,128)S(1)} collective-permute-done((f32[32,128]{1,0:T(8,128)S(1)}, f32[32,128]{1,0:T(8,128)S(1)}, u32[]{:S(2)}, u32[]{:S(2)}) %collective-permute-start.6) | collective-permute-done | bytes 16416 | tf_op jit(solution)/shard_map/ppermute | solution.py:53
  72.8 31.8 %all-gather.1 = f32[1024,128]{1,0:T(8,128)S(1)} all-gather(f32[32,128]{1,0:T(8,128)S(1)} %add.64), channel_id=3, replica_groups=mesh['col'=32,'sub'=8] {'col'}, dimensions={0}, use_global_device_ids=true | all-gather | bytes 540672 | tf_op jit(solution)/shard_map/all_gather | solution.py:54
  104.6 0.6 gather_fusion.3
  105.2 0.0 copy-done.4
  105.2 1.0 convolution_bitcast_fusion.2
  106.2 0.9 fusion.4
  107.1 0.0 collective-permute-done.3
  107.1 0.0 collective-permute-done.2
  107.1 1.0 pad_maximum_fusion.1
  108.1 2.1 %gather_fusion.1 = f32[128,32,128]{2,1,0:T(8,128)} fusion(f32[48,32,128]{2,1,0:T(8,128)S(1)} %pad_maximum_fusion.1, s32[1024]{0:T(1024)S(1)} %pad_clamp_fusion.2), kind=kCustom, calls=%fused_computation.1 | custom fusion | bytes 4194816 | tf_op jit(solution)/shard_map/gather | solution.py:59
  110.2 0.0 copy-done
  110.3 4.4 %convolution_bitcast_fusion.1 = f32[16,32,128]{2,1,0:T(8,128)S(1)} fusion(f32[16,8,32,128]{3,2,1,0:T(8,128)} %bitcast.77, f32[16,8,32,32]{3,2,1,0:T(8,128)S(1)} %copy-done), kind=kOutput, calls=%fused_computation.10 | convolution fusion | flops 201326592 | bytes 2883584 | tf_op jit(solution)/shard_map/lkrs,lksc->lrc/dot_general | solution.py:60
  114.7 0.0 copy-done.3
  114.7 0.4 fusion.3
  115.1 0.0 copy-done.2
  115.1 1.9 %fusion.14 = f32[16,128,256]{2,1,0:T(8,128)} fusion(bf16[16,32,128]{2,1,0:T(8,128)(2,1)S(1)} %fusion.3, bf16[16,32,256]{2,1,0:T(8,128)(2,1)S(1)} %copy-done.2), kind=kOutput, calls=%fused_computation.35 | convolution fusion | flops 33554432 | bytes 2490368 | tf_op jit(solution)/shard_map/lrp,lrc->lpc/dot_general | solution.py:69
  117.0 0.0 collective-permute-done.1
  117.0 0.0 collective-permute-done
  117.0 0.0 copy-done.1
  117.0 9.8 %pad_maximum_fusion = bf16[12288,128]{1,0:T(8,128)(2,1)} fusion(bf16[4096,128]{1,0:T(8,128)(2,1)} %collective-permute-done.1, bf16[4096,128]{1,0:T(8,128)(2,1)S(1)} %copy-done.1, bf16[4096,128]{1,0:T(8,128)(2,1)} %collective-permute-done), kind=kLoop, calls=%fused_computation.4 | loop fusion | flops 9437184 | bytes 6291456 | tf_op jit(solution)/shard_map/concatenate | solution.py:18
  126.8 4.9 %gather_fusion = bf16[64,256,128]{2,1,0:T(8,128)(2,1)} fusion(bf16[48,256,128]{2,1,0:T(8,128)(2,1)} %bitcast.75, s32[1024]{0:T(1024)S(1)} %pad_clamp_fusion.3), kind=kCustom, calls=%fused_computation | custom fusion | bytes 8388864 | tf_op jit(solution)/shard_map/gather | solution.py:65
  131.7 8.1 %fusion.1 = bf16[16,256,128]{1,2,0:T(8,128)(2,1)S(1)} fusion(f32[16,128,256]{2,1,0:T(8,128)} %fusion.14, bf16[16,4,256,128]{3,2,1,0:T(8,128)(2,1)} %bitcast.76, bf16[16,4,256,256]{3,2,1,0:T(8,128)(2,1)} %param.13), kind=kOutput, calls=%fused_computation.7 | convolution fusion | flops 1074790400 | bytes 15728640 | tf_op jit(solution)/shard_map/lkij,lkjc->lic/dot_general | solution.py:66
  139.8 1.3 copy.21
  (10 shorter events, 0.0 us)
Async XLA Ops:
  0.0 110.2 %copy-start = (f32[16,8,32,32]{3,2,1,0:T(8,128)S(1)}, f32[16,8,32,32]{3,2,1,0:T(8,128)}, u32[]{:S(2)}) copy-start(f32[16,8,32,32]{3,2,1,0:T(8,128)} %param.17) | copy-start | bytes 1572868
  0.0 105.2 %copy-start.4 = (f32[1,8,32,32]{3,2,1,0:T(8,128)S(1)}, f32[1,8,32,32]{3,2,1,0:T(8,128)}, u32[]{:S(2)}) copy-start(f32[1,8,32,32]{3,2,1,0:T(8,128)} %param.22) | copy-start | bytes 98308
  1.7 105.4 %collective-permute-start.3 = (f32[16,32,128]{2,1,0:T(8,128)S(1)}, f32[16,32,128]{2,1,0:T(8,128)S(1)}, u32[]{:S(2)}, u32[]{:S(2)}) collective-permute-start(f32[16,32,128]{2,1,0:T(8,128)S(1)} %fusion.12), channel_id=1, source_target_pairs={{1,0},{2,1},{3,2},{4,3},{5,4},{6,5},{7,6},{8,7},{9,8},{10,9},{11,1... | collective-permute-start | bytes 786440 | tf_op jit(solution)/shard_map/ppermute | solution.py:17
  10.6 96.5 %collective-permute-start.2 = (f32[16,32,128]{2,1,0:T(8,128)S(1)}, f32[16,32,128]{2,1,0:T(8,128)}, u32[]{:S(2)}, u32[]{:S(2)}) collective-permute-start(f32[16,32,128]{2,1,0:T(8,128)S(1)} %fusion.12), channel_id=1, source_target_pairs={{0,1},{1,2},{2,3},{3,4},{4,5},{5,6},{6,7},{7,8},{8,9},{9,10},{10,1... | collective-permute-start | bytes 786440 | tf_op jit(solution)/shard_map/ppermute | solution.py:14
  12.5 104.4 %collective-permute-start.1 = (bf16[4096,128]{1,0:T(8,128)(2,1)}, bf16[4096,128]{1,0:T(8,128)(2,1)}, u32[]{:S(2)}, u32[]{:S(2)}) collective-permute-start(bf16[4096,128]{1,0:T(8,128)(2,1)} %param.12), channel_id=1, source_target_pairs={{1,0},{2,1},{3,2},{4,3},{5,4},{6,5},{7,6},{8,7},{9,8},{10,9},{11,1... | collective-permute-start | bytes 3145736 | tf_op jit(solution)/shard_map/ppermute | solution.py:17
  17.4 99.6 %collective-permute-start = (bf16[4096,128]{1,0:T(8,128)(2,1)}, bf16[4096,128]{1,0:T(8,128)(2,1)}, u32[]{:S(2)}, u32[]{:S(2)}) collective-permute-start(bf16[4096,128]{1,0:T(8,128)(2,1)} %param.12), channel_id=1, source_target_pairs={{0,1},{1,2},{2,3},{3,4},{4,5},{5,6},{6,7},{7,8},{8,9},{9,10},{10,1... | collective-permute-start | bytes 3145736 | tf_op jit(solution)/shard_map/ppermute | solution.py:14
  21.8 40.9 %collective-permute-start.4 = (f32[32,128]{1,0:T(8,128)S(1)}, f32[32,128]{1,0:T(8,128)S(1)}, u32[]{:S(2)}, u32[]{:S(2)}) collective-permute-start(f32[32,128]{1,0:T(8,128)S(1)} %convolution_bitcast_fusion.4), channel_id=1, source_target_pairs={{0,1},{1,0},{2,3},{3,2},{4,5},{5,4},{6,7},{7,6},{8,9},{9,8},{10,11... | collective-permute-start | bytes 49160 | tf_op jit(solution)/shard_map/ppermute | solution.py:53
  62.7 3.6 %collective-permute-start.5 = (f32[32,128]{1,0:T(8,128)S(1)}, f32[32,128]{1,0:T(8,128)S(1)}, u32[]{:S(2)}, u32[]{:S(2)}) collective-permute-start(f32[32,128]{1,0:T(8,128)S(1)} %add.62), channel_id=1, source_target_pairs={{0,2},{1,3},{2,0},{3,1},{4,6},{5,7},{6,4},{7,5},{8,10},{9,11},{10,... | collective-permute-start | bytes 49160 | tf_op jit(solution)/shard_map/ppermute | solution.py:53
  66.3 6.5 %collective-permute-start.6 = (f32[32,128]{1,0:T(8,128)S(1)}, f32[32,128]{1,0:T(8,128)S(1)}, u32[]{:S(2)}, u32[]{:S(2)}) collective-permute-start(f32[32,128]{1,0:T(8,128)S(1)} %add.63), channel_id=1, source_target_pairs={{0,4},{1,5},{2,6},{3,7},{4,0},{5,1},{6,2},{7,3},{8,12},{9,13},{10,... | collective-permute-start | bytes 49160 | tf_op jit(solution)/shard_map/ppermute | solution.py:53
  110.2 4.4 %copy-start.3 = (f32[16,32,32]{2,1,0:T(8,128)S(1)}, f32[16,32,32]{2,1,0:T(8,128)}, u32[]{:S(2)}) copy-start(f32[16,32,32]{2,1,0:T(8,128)} %param.16) | copy-start | bytes 196612
  110.2 4.8 %copy-start.2 = (bf16[16,32,256]{2,1,0:T(8,128)(2,1)S(1)}, bf16[16,32,256]{2,1,0:T(8,128)(2,1)}, u32[]{:S(2)}) copy-start(bf16[16,32,256]{2,1,0:T(8,128)(2,1)} %param.15) | copy-start | bytes 786436
  110.2 6.7 %copy-start.1 = (bf16[4096,128]{1,0:T(8,128)(2,1)S(1)}, bf16[4096,128]{1,0:T(8,128)(2,1)}, u32[]{:S(2)}) copy-start(bf16[4096,128]{1,0:T(8,128)(2,1)} %param.12) | copy-start | bytes 3145732
